TPU v7x, 32 devices: a whole 2x2x4 slice. The times are simulated.
32 devices in a mesh: row: 4 (over y, core), col: 8 (over z, x).
Axes of the slice: x: 2, y: 2, z: 4, core: 2. Of those that a mesh axis runs over, the one named last changes fastest.
Arguments:
- ancestor_inverse: float32 [12288, 12288], P('row', 'col')
- factor: bfloat16 [3, 12288, 512], P(None, ('row', 'col')), may hold values from -0.5 to 0.5
- coupling: float32 [3, 512, 512], replicated, may hold values from -0.25 to 0.25
- diagonal_inverse: float32 [3, 512, 512], replicated, may hold values from -6 to 6
- ancestors: int32 [3, 24], replicated, may hold values from -1 to 23, as said below
Outputs:
- block_columns: float32 [3, 12288, 512], P(None, ('row', 'col'))
- block_rows: float32 [3, 12288, 512], P(None, ('col', 'row'))
- node_blocks: float32 [3, 3, 512, 512], replicated
Inputs may be any that keep to these rules, and one draw needn't show every extreme that they name: `ancestors`: row k lists the ancestor block rows of supernode k, blocks of 512 rows: distinct indices in increasing order, then -1 in the slots left. Every block is listed by some supernode.
All inputs are finite; a program needn't handle non-finite values.
Results may differ from a plain program's by a relative error of at most 0.0003.
Values may be sent and summed in bfloat16 or wider, within the bound.
No kernel may reach another device: no remote copies, remote signals or barrier semaphores. Data moves between devices by JAX's collectives and lax.ppermute only.
A program may use at most 128 MiB of HBM per device.

v0:
```python
import jax
import jax.numpy as jnp
from jax import lax
from jax.sharding import PartitionSpec as P

highest = lax.Precision.HIGHEST


def broadcast(value, axis, source):
    kept = jnp.where(lax.axis_index(axis) == source, value, 0).astype(value.dtype)
    return lax.psum(kept, axis)


def matmul(left, right):
    return jnp.dot(left, right, precision=highest)


def left_dot(left, right):
    return lax.dot_general(left, right, (((0,), (0,)), ((), ())), precision=highest)


def pair_index(later, earlier):
    return later * (later - 1) // 2 + earlier


def local(ancestor_inverse, factor, coupling, diagonal_inverse, ancestors):
    col_count = lax.axis_size("col")
    row_index = lax.axis_index("row")
    col_index = lax.axis_index("col")
    nodes_total, piece_rows, sn_width = factor.shape
    rows_here, cols_here = ancestor_inverse.shape
    group_ratio = rows_here // cols_here
    first_row = (row_index * col_count + col_index) * piece_rows
    block_of_row = (first_row + jnp.arange(piece_rows, dtype=jnp.int32)) // sn_width
    source_row = col_index // group_ratio
    block_start = col_index % group_ratio * cols_here
    row_layout = []
    col_layout = []
    solved = {}
    for current in range(nodes_total):
        listed = jnp.any(ancestors[current][:, None] == block_of_row[None, :], axis=0)
        lower_part = jnp.where(listed[:, None], factor[current], jnp.zeros_like(factor[current]))
        lower_rows = lax.all_gather(lower_part, "col", axis=0, tiled=True)
        own_block = lax.dynamic_slice_in_dim(lower_rows, block_start, cols_here, 0)
        lower_cols = broadcast(own_block, "row", source_row).astype(jnp.float32)
        lower_here = lower_part.astype(jnp.float32)
        product_sum = lax.psum_scatter(
            matmul(ancestor_inverse, lower_cols), "col", scatter_dimension=0, tiled=True
        )
        for earlier in range(current):
            product_sum = product_sum + matmul(
                row_layout[earlier], coupling[pair_index(current, earlier)]
            )
        column = -product_sum
        stacked = jnp.concatenate(row_layout + [column], axis=1)
        summed = lax.psum(left_dot(lower_here, stacked), ("row", "col"))
        crosses = [
            summed[:, earlier * sn_width : (earlier + 1) * sn_width] for earlier in range(current)
        ]
        self_term = summed[:, current * sn_width : (current + 1) * sn_width]
        for earlier in range(current):
            block_value = -crosses[earlier].T
            for inner in range(current):
                block_value = block_value - matmul(
                    solved[earlier, inner], coupling[pair_index(current, inner)]
                )
            solved[earlier, current] = block_value
            solved[current, earlier] = block_value.T
        diag_value = diagonal_inverse[current] - self_term
        for earlier in range(current):
            diag_value = diag_value - left_dot(
                coupling[pair_index(current, earlier)], solved[earlier, current]
            )
        solved[current, current] = diag_value
        rows_float = lower_rows.astype(jnp.float32)
        mirror = lax.psum_scatter(
            left_dot(ancestor_inverse, rows_float), "row", scatter_dimension=0, tiled=True
        )
        for earlier in range(current):
            mirror = mirror + matmul(col_layout[earlier], coupling[pair_index(current, earlier)])
        col_layout.append(-mirror)
        row_layout.append(column)
    finished = jnp.stack(row_layout)
    mirrored_all = jnp.stack(col_layout)
    node_blocks = jnp.stack(
        [
            jnp.stack([solved[first_node, second_node] for second_node in range(nodes_total)])
            for first_node in range(nodes_total)
        ]
    )
    return (finished, mirrored_all, node_blocks)


def solution(mesh):
    placed = (P("row", "col"), P(None, ("row", "col"), None), P(), P(), P())
    return jax.shard_map(
        local,
        mesh=mesh,
        in_specs=placed,
        out_specs=(P(None, ("row", "col"), None), P(None, ("col", "row"), None), P()),
        check_vma=False,
    )
```

profile of v0, /device:TPU:0, one launch (start us, length us, event | category | flops | bytes accessed | tf_op | source)
XLA Modules:
  0.0 1007.5 jit_solution(5974017174490358877)
XLA Ops:
  8.1 2.5 bitcast_select_fusion.1
  12.2 61.3 %all-gather.8.cloned.1.call-done = bf16[3072,512]{1,0:T(8,128)(2,1)} async-done(((bf16[384,512]{1,0:T(8,128)(2,1)}), bf16[3072,512]{1,0:T(8,128)(2,1)}) %all-gather.8.cloned.1.call-update) | async-done | bytes 3145744 | tf_op jit(solution)/shard_map/all_gather | solution.py:43
  73.6 2.8 dynamic-slice_select_fusion
  76.4 58.1 %all-gather.4.cloned.1.call-done = bf16[3072,512]{1,0:T(8,128)(2,1)} async-done(((bf16[384,512]{1,0:T(8,128)(2,1)}), bf16[3072,512]{1,0:T(8,128)(2,1)}) %all-gather.4.cloned.1.call-update) | async-done | bytes 3145744 | tf_op jit(solution)/shard_map/all_gather | solution.py:43
  134.5 2.8 dynamic-slice_select_fusion.2
  137.3 58.1 %all-gather.6.cloned.1.call-done = bf16[3072,512]{1,0:T(8,128)(2,1)} async-done(((bf16[384,512]{1,0:T(8,128)(2,1)}), bf16[3072,512]{1,0:T(8,128)(2,1)}) %all-gather.6.cloned.1.call-update) | async-done | bytes 3145744 | tf_op jit(solution)/shard_map/all_gather | solution.py:43
  195.4 2.8 dynamic-slice_select_fusion.1
  198.3 92.8 %all-reduce.7.cloned.1.call-done = (bf16[1536,512]{1,0:T(8,128)(2,1)}, bf16[1536,512]{1,0:T(8,128)(2,1)}, bf16[1536,512]{1,0:T(8,128)(2,1)}) async-done(((bf16[1536,512]{1,0:T(8,128)(2,1)}, bf16[1536,512]{1,0:T(8,128)(2,1)}, bf16[1536,512]{1,0:T(8,128)(2,1)}), (bf16[1536,512]{1,0:T(8,128)(2,1)}, bf16[1536,512]{1,0:T(8,128)(2,1)}, bf16[1536,512]{1,0:T(8,128)(2,1)})) %all-reduce.7.cloned.1.call-update) | async-done | bytes 4718608 | tf_op jit(solution)/shard_map/psum | solution.py:11
  291.1 22.4 %convolution_bitcast_fusion.2 = f32[3072,512]{0,1:T(8,128)} fusion(bf16[1536,512]{1,0:T(8,128)(2,1)} %get-tuple-element.16, f32[3072,1536]{1,0:T(8,128)} %param.5), kind=kOutput, calls=%fused_computation.3 | convolution fusion | flops 28991029248 | bytes 26738688 | tf_op jit(solution)/shard_map/dot_general | solution.py:15
  314.9 21.8 %convolution_bitcast_fusion.1 = f32[3072,512]{0,1:T(8,128)} fusion(bf16[1536,512]{1,0:T(8,128)(2,1)S(1)} %copy-done.30, f32[3072,1536]{1,0:T(8,128)} %param.5), kind=kOutput, calls=%fused_computation.2 | convolution fusion | flops 28991029248 | bytes 26738688 | tf_op jit(solution)/shard_map/dot_general | solution.py:15
  338.1 21.8 %convolution_bitcast_fusion = f32[3072,512]{0,1:T(8,128)} fusion(bf16[1536,512]{1,0:T(8,128)(2,1)S(1)} %copy-done.29, f32[3072,1536]{1,0:T(8,128)} %param.5), kind=kOutput, calls=%fused_computation.1 | convolution fusion | flops 28991029248 | bytes 26738688 | tf_op jit(solution)/shard_map/dot_general | solution.py:15
  361.8 19.7 %convolution_bitcast_fusion.3 = f32[1536,512]{0,1:T(8,128)} fusion(bf16[3072,512]{1,0:T(8,128)(2,1)S(1)} %copy-done.28, f32[3072,1536]{1,0:T(8,128)} %param.5), kind=kOutput, calls=%fused_computation.4 | convolution fusion | flops 28991029248 | bytes 25165824 | tf_op jit(solution)/shard_map/dot_general | solution.py:19
  383.5 19.9 %convolution_bitcast_fusion.5 = f32[1536,512]{0,1:T(8,128)} fusion(bf16[3072,512]{1,0:T(8,128)(2,1)S(1)} %copy-done.27, f32[3072,1536]{1,0:T(8,128)} %param.5), kind=kOutput, calls=%fused_computation.6 | convolution fusion | flops 28991029248 | bytes 25165824 | tf_op jit(solution)/shard_map/dot_general | solution.py:19
  405.3 19.7 %convolution_bitcast_fusion.4 = f32[1536,512]{0,1:T(8,128)} fusion(bf16[3072,512]{1,0:T(8,128)(2,1)S(1)} %copy-done.26, f32[3072,1536]{1,0:T(8,128)} %param.5), kind=kOutput, calls=%fused_computation.5 | convolution fusion | flops 28991029248 | bytes 25165824 | tf_op jit(solution)/shard_map/dot_general | solution.py:19
  425.3 6.5 reduce-scatter.7.cloned.1.call-done
  431.8 2.4 fusion.73
  434.2 3.3 fusion.64
  437.5 115.1 %reduce-scatter.9.cloned.1.call-done = f32[384,512]{0,1:T(8,128)} async-done(((f32[3072,512]{0,1:T(8,128)}), f32[384,512]{0,1:T(8,128)}) %reduce-scatter.9.cloned.1.call-update) | async-done | bytes 786448 | tf_op jit(solution)/shard_map/reduce_scatter | solution.py:47
  552.6 3.4 fusion.14
  556.9 3.1 fusion.6
  560.0 114.0 %reduce-scatter.11.cloned.1.call-done = f32[384,512]{0,1:T(8,128)} async-done(((f32[3072,512]{0,1:T(8,128)}), f32[384,512]{0,1:T(8,128)}) %reduce-scatter.11.cloned.1.call-update) | async-done | bytes 786448 | tf_op jit(solution)/shard_map/reduce_scatter | solution.py:47
  674.0 3.3 convolution_add_fusion.4
  680.2 4.5 fusion
  684.7 2.3 slice.74
  687.0 2.9 copy.65
  690.0 23.6 %reduce-scatter.17.cloned.1.call-done = f32[384,512]{0,1:T(8,128)} async-done(((f32[1536,512]{0,1:T(8,128)}), f32[384,512]{0,1:T(8,128)}) %reduce-scatter.17.cloned.1.call-update) | async-done | bytes 786448 | tf_op jit(solution)/shard_map/reduce_scatter | solution.py:76
  713.6 40.3 %reduce-scatter.13.cloned.1.call-done = f32[384,512]{0,1:T(8,128)} async-done(((f32[1536,512]{0,1:T(8,128)}), f32[384,512]{0,1:T(8,128)}) %reduce-scatter.13.cloned.1.call-update) | async-done | bytes 786448 | tf_op jit(solution)/shard_map/reduce_scatter | solution.py:76
  753.9 4.1 convolution_add_fusion.1
  758.0 36.0 %reduce-scatter.15.cloned.1.call-done = f32[384,512]{0,1:T(8,128)} async-done(((f32[1536,512]{0,1:T(8,128)}), f32[384,512]{0,1:T(8,128)}) %reduce-scatter.15.cloned.1.call-update) | async-done | bytes 786448 | tf_op jit(solution)/shard_map/reduce_scatter | solution.py:76
  794.0 3.4 fusion.16
  800.9 3.0 copy.51
  804.0 3.2 pad_maximum_fusion.1
  807.1 3.2 copy.50
  810.3 146.5 %all-reduce.5.cloned.1.call-done = (f32[512,1536]{1,0:T(8,128)}, f32[512,512]{1,0:T(8,128)}, f32[512,1024]{0,1:T(8,128)}) async-done(((f32[512,1536]{1,0:T(8,128)}, f32[512,512]{1,0:T(8,128)}, f32[512,1024]{0,1:T(8,128)}), (f32[512,1536]{1,0:T(8,128)}, f32[512,512]{1,0:T(8,128)}, f32[512,1024]{0,1:T(8,128)})) %all-reduce.5.cloned.1.call-update) | async-done | bytes 6291472 | tf_op jit(solution)/shard_map/psum | solution.py:56
  956.9 3.6 fusion.34
  960.5 3.2 bitcast_subtract_fusion.7
  963.7 1.9 fusion.32
  967.5 2.0 fusion.13
  970.5 1.9 fusion.25
  972.4 3.3 fusion.12
  975.7 2.3 fusion.20
  978.0 2.3 fusion.70
  980.3 2.5 copy.39
  982.9 5.3 fusion.11
  988.2 2.0 maximum_bitcast_fusion.1
  990.1 2.4 copy.49
  992.6 2.3 maximum_bitcast_fusion.2
  995.6 5.1 pad_maximum_fusion
  (93 shorter events, 22.2 us)
Async XLA Ops:
  7.2 66.4 %all-gather.8.cloned.1.call-start = ((), (), s32[]{:S(2)}) async-start(), calls=%async_computation.10 | async-start | bytes 3538944 | tf_op jit(solution)/shard_map/all_gather | solution.py:43
  10.7 123.8 %all-gather.4.cloned.1.call-start = ((), (), s32[]{:S(2)}) async-start(), calls=%async_computation.6 | async-start | bytes 3538944 | tf_op jit(solution)/shard_map/all_gather | solution.py:43
  11.4 183.9 %all-gather.6.cloned.1.call-start = ((), (), s32[]{:S(2)}) async-start(), calls=%async_computation.8 | async-start | bytes 3538944 | tf_op jit(solution)/shard_map/all_gather | solution.py:43
  12.2 278.9 %all-reduce.7.cloned.1.call-start = ((), (), s32[]{:S(2)}) async-start(), calls=%async_computation.16 | async-start | bytes 9437184 | tf_op jit(solution)/shard_map/psum | solution.py:11
  198.2 233.6 %reduce-scatter.7.cloned.1.call-start = ((), (), s32[]{:S(2)}) async-start(), calls=%async_computation.7 | async-start | bytes 7077888 | tf_op jit(solution)/shard_map/reduce_scatter | solution.py:47
  313.5 1.4 copy-start.30
  313.5 239.1 %reduce-scatter.9.cloned.1.call-start = ((), (), s32[]{:S(2)}) async-start(), calls=%async_computation.9 | async-start | bytes 7077888 | tf_op jit(solution)/shard_map/reduce_scatter | solution.py:47
  336.7 1.4 copy-start.29
  336.7 337.3 %reduce-scatter.11.cloned.1.call-start = ((), (), s32[]{:S(2)}) async-start(), calls=%async_computation.11 | async-start | bytes 7077888 | tf_op jit(solution)/shard_map/reduce_scatter | solution.py:47
  359.9 1.9 copy-start.28
  359.9 353.6 %reduce-scatter.17.cloned.1.call-start = ((), (), s32[]{:S(2)}) async-start(), calls=%async_computation.14 | async-start | bytes 3932160 | tf_op jit(solution)/shard_map/reduce_scatter | solution.py:76
  381.6 2.0 copy-start.27
  381.6 372.2 %reduce-scatter.13.cloned.1.call-start = ((), (), s32[]{:S(2)}) async-start(), calls=%async_computation.12 | async-start | bytes 3932160 | tf_op jit(solution)/shard_map/reduce_scatter | solution.py:76
  403.4 1.9 copy-start.26
  403.5 390.5 %reduce-scatter.15.cloned.1.call-start = ((), (), s32[]{:S(2)}) async-start(), calls=%async_computation.13 | async-start | bytes 3932160 | tf_op jit(solution)/shard_map/reduce_scatter | solution.py:76
  425.0 9.2 copy-start.23
  425.0 127.6 %copy-start = (f32[3,512,512]{2,1,0:T(8,128)S(1)}, f32[3,512,512]{2,1,0:T(8,128)}, u32[]{:S(2)}) copy-start(f32[3,512,512]{2,1,0:T(8,128)} %param.7) | copy-start | bytes 9437188
  425.0 531.9 %all-reduce.5.cloned.1.call-start = ((), (), s32[]{:S(2)}) async-start(), calls=%async_computation.15 | async-start | bytes 12582912 | tf_op jit(solution)/shard_map/psum | solution.py:56
  437.5 119.4 %copy-start.24 = (bf16[384,512]{1,0:T(8,128)(2,1)S(1)}, bf16[384,512]{1,0:T(8,128)(2,1)}, u32[]{:S(2)}) copy-start(bf16[384,512]{1,0:T(8,128)(2,1)} %get-tuple-element.22) | copy-start | bytes 1179652
  552.6 4.3 copy-start.13
  555.9 0.9 copy-start.3
  560.0 120.2 %copy-start.16 = (bf16[384,512]{1,0:T(8,128)(2,1)S(1)}, bf16[384,512]{1,0:T(8,128)(2,1)}, u32[]{:S(2)}) copy-start(bf16[384,512]{1,0:T(8,128)(2,1)} %get-tuple-element.24) | copy-start | bytes 1179652
  674.0 3.4 copy-start.4
  674.0 6.2 copy-start.14
  679.2 0.9 copy-start.12
  794.0 3.4 copy-start.25
  794.0 5.3 copy-start.15
  956.9 3.6 copy-start.10
  956.9 3.6 copy-start.11
  963.7 3.8 copy-start.1
  963.7 3.8 copy-start.17
  963.7 3.8 copy-start.18
  965.6 12.4 %copy-start.5 = (f32[512,512]{0,1:T(8,128)}, f32[512,512]{0,1:T(8,128)S(1)}, u32[]{:S(2)}) copy-start(f32[512,512]{0,1:T(8,128)S(1)} %fusion.32) | copy-start | bytes 3145732
  967.5 4.9 copy-start.7
  969.5 1.0 copy-start.8
  972.4 5.6 copy-start.6
  982.9 5.3 copy-start.9
  982.9 5.3 copy-start.21
  982.9 5.3 copy-start.22
  992.5 2.4 copy-start.2
  992.5 2.5 copy-start.19
  992.5 2.8 copy-start.20
Sparse Core Ops, SparseCore 0:
  10.8 62.7 all-gather.7
  75.7 58.6 all-gather.3
  136.7 58.6 all-gather.5
  198.3 92.7 all-reduce.6
  313.6 118.1 reduce-scatter.6
  435.2 117.2 reduce-scatter.8
  556.7 117.2 reduce-scatter.10
  676.5 36.9 reduce-scatter.16
  716.1 37.7 reduce-scatter.12
  756.2 37.7 reduce-scatter.14
  800.5 156.3 all-reduce.4
where the time goes:
time: 1020 us; the launch traced here: 1010 us
  waiting for transfers between devices  754 us (74%)
  matrix products  177 us (17%)
  other arithmetic  32.6 us (3%)
  local copies, waits for them, and re-layouts  28.1 us (3%)
  between operations  14.5 us (1%)
    reduce_scatter x3, waiting for transfers between devices, local(): lax.psum_scatter(matmul(ancestor_inverse, lower_cols), 'col', scatter_dim...  236 us
    all_gather x3, waiting for transfers between devices, local(): lower_rows = lax.all_gather(lower_part, 'col', axis=0, tiled=True)  177 us
    psum x1, waiting for transfers between devices, local(): summed = lax.psum(left_dot(lower_here, stacked), ('row', 'col'))  147 us
    reduce_scatter x3, waiting for transfers between devices, local(): lax.psum_scatter(left_dot(ancestor_inverse, rows_float), 'row', scatter_d...  99.9 us
    dot_general x14, matrix products, matmul(): return jnp.dot(left, right, precision=highest)  96.3 us
    psum x1, waiting for transfers between devices, broadcast(): return lax.psum(kept, axis)  92.8 us
    dot_general x9, matrix products, left_dot(): lax.dot_general(left, right, (((0,), (0,)), ((), ())), precision=highest)  80.7 us
  transfers between devices with their start and end apart: 11, of which 11 were waited for; matrix products, arithmetic and copies ran while one was open for 15% of the time, Pallas kernels for 0%

commit v1 on v0

--- a/solution.py
+++ b/solution.py
@@ -53,7 +53,7 @@
             )
         column = -product_sum
         stacked = jnp.concatenate(row_layout + [column], axis=1)
-        summed = lax.psum(left_dot(lower_here, stacked), ("row", "col"))
+        summed = lax.psum(lax.psum(left_dot(lower_here, stacked), "col"), "row")
         crosses = [
             summed[:, earlier * sn_width : (earlier + 1) * sn_width] for earlier in range(current)
         ]

time: 1020 us -> 1200 us (1.18)
  waiting for transfers between devices: 754 us -> 934 us
    psum x1 -> x2, waiting for transfers between devices: 147 us -> 251 us  [local(): summed = lax.psum(lax.psum(left_dot(lower_here, stacked), 'col'), 'row')]
    reduce_scatter x3, waiting for transfers between devices: 236 us -> 299 us  [local(): lax.psum_scatter(matmul(ancestor_inverse, lower_cols), 'col', scatter_dim...]
  transfers between devices with their start and end apart: 11 -> 12, of which waited for: 11 -> 12; matrix products, arithmetic and copies ran while one was open for 15% -> 12% of each run, Pallas kernels for 0% -> 0%
where the time goes in v1:
time: 1200 us; the launch traced here: 1190 us
  waiting for transfers between devices  934 us (78%)
  matrix products  180 us (15%)
  other arithmetic  31.1 us (3%)
  local copies, waits for them, and re-layouts  20.3 us (2%)
  between operations  15 us (1%)
  starting transfers between devices  12.7 us (1%)
    reduce_scatter x3, waiting for transfers between devices, local(): lax.psum_scatter(matmul(ancestor_inverse, lower_cols), 'col', scatter_dim...  299 us
    psum x2, waiting for transfers between devices, local(): summed = lax.psum(lax.psum(left_dot(lower_here, stacked), 'col'), 'row')  251 us
    all_gather x3, waiting for transfers between devices, local(): lower_rows = lax.all_gather(lower_part, 'col', axis=0, tiled=True)  177 us
    reduce_scatter x3, waiting for transfers between devices, local(): lax.psum_scatter(left_dot(ancestor_inverse, rows_float), 'row', scatter_d...  111 us
    dot_general x14, matrix products, matmul(): return jnp.dot(left, right, precision=highest)  97.1 us
    psum x1, waiting for transfers between devices, broadcast(): return lax.psum(kept, axis)  92.8 us
    dot_general x9, matrix products, left_dot(): lax.dot_general(left, right, (((0,), (0,)), ((), ())), precision=highest)  82.8 us
  transfers between devices with their start and end apart: 12, of which 12 were waited for; matrix products, arithmetic and copies ran while one was open for 12% of the time, Pallas kernels for 0%

profile of v1, /device:TPU:0, one launch (start us, length us, event | category | flops | bytes accessed | tf_op | source)
XLA Modules:
  0.0 1192.6 jit_solution(3969772240734581204)
XLA Ops:
  8.1 2.5 bitcast_select_fusion.1
  12.2 61.3 %all-gather.8.cloned.1.call-done = bf16[3072,512]{1,0:T(8,128)(2,1)} async-done(((bf16[384,512]{1,0:T(8,128)(2,1)}), bf16[3072,512]{1,0:T(8,128)(2,1)}) %all-gather.8.cloned.1.call-update) | async-done | bytes 3145744 | tf_op jit(solution)/shard_map/all_gather | solution.py:43
  73.5 2.8 dynamic-slice_select_fusion
  76.3 58.1 %all-gather.4.cloned.1.call-done = bf16[3072,512]{1,0:T(8,128)(2,1)} async-done(((bf16[384,512]{1,0:T(8,128)(2,1)}), bf16[3072,512]{1,0:T(8,128)(2,1)}) %all-gather.4.cloned.1.call-update) | async-done | bytes 3145744 | tf_op jit(solution)/shard_map/all_gather | solution.py:43
  134.4 2.8 dynamic-slice_select_fusion.2
  137.2 58.1 %all-gather.6.cloned.1.call-done = bf16[3072,512]{1,0:T(8,128)(2,1)} async-done(((bf16[384,512]{1,0:T(8,128)(2,1)}), bf16[3072,512]{1,0:T(8,128)(2,1)}) %all-gather.6.cloned.1.call-update) | async-done | bytes 3145744 | tf_op jit(solution)/shard_map/all_gather | solution.py:43
  195.3 2.8 dynamic-slice_select_fusion.1
  198.2 92.8 %all-reduce.11.cloned.1.call-done = (bf16[1536,512]{1,0:T(8,128)(2,1)}, bf16[1536,512]{1,0:T(8,128)(2,1)}, bf16[1536,512]{1,0:T(8,128)(2,1)}) async-done(((bf16[1536,512]{1,0:T(8,128)(2,1)}, bf16[1536,512]{1,0:T(8,128)(2,1)}, bf16[1536,512]{1,0:T(8,128)(2,1)}), (bf16[1536,512]{1,0:T(8,128)(2,1)}, bf16[1536,512]{1,0:T(8,128)(2,1)}, bf16[1536,512]{1,0:T(8,128)(2,1)})) %all-reduce.11.cloned.1.call-update) | async-done | bytes 4718608 | tf_op jit(solution)/shard_map/psum | solution.py:11
  291.0 22.2 %convolution_bitcast_fusion = f32[3072,512]{0,1:T(8,128)} fusion(bf16[1536,512]{1,0:T(8,128)(2,1)} %get-tuple-element.18, f32[3072,1536]{1,0:T(8,128)} %param.5), kind=kOutput, calls=%fused_computation.1 | convolution fusion | flops 28991029248 | bytes 26738688 | tf_op jit(solution)/shard_map/dot_general | solution.py:15
  314.7 21.8 %convolution_bitcast_fusion.2 = f32[3072,512]{0,1:T(8,128)} fusion(bf16[1536,512]{1,0:T(8,128)(2,1)S(1)} %copy-done.26, f32[3072,1536]{1,0:T(8,128)} %param.5), kind=kOutput, calls=%fused_computation.3 | convolution fusion | flops 28991029248 | bytes 26738688 | tf_op jit(solution)/shard_map/dot_general | solution.py:15
  336.5 11.7 reduce-scatter.9.cloned.1.call-start
  348.3 21.9 %convolution_bitcast_fusion.1 = f32[3072,512]{0,1:T(8,128)} fusion(bf16[1536,512]{1,0:T(8,128)(2,1)S(1)} %copy-done.25, f32[3072,1536]{1,0:T(8,128)} %param.5), kind=kOutput, calls=%fused_computation.2 | convolution fusion | flops 28991029248 | bytes 26738688 | tf_op jit(solution)/shard_map/dot_general | solution.py:15
  370.2 61.4 %reduce-scatter.11.cloned.1.call-done = f32[384,512]{0,1:T(8,128)} async-done(((f32[3072,512]{0,1:T(8,128)}), f32[384,512]{0,1:T(8,128)}) %reduce-scatter.11.cloned.1.call-update) | async-done | bytes 786448 | tf_op jit(solution)/shard_map/reduce_scatter | solution.py:47
  431.6 120.7 %reduce-scatter.7.cloned.1.call-done = f32[384,512]{0,1:T(8,128)} async-done(((f32[3072,512]{0,1:T(8,128)}), f32[384,512]{0,1:T(8,128)}) %reduce-scatter.7.cloned.1.call-update) | async-done | bytes 786448 | tf_op jit(solution)/shard_map/reduce_scatter | solution.py:47
  552.4 4.1 convolution_add_fusion.4
  556.5 116.8 %reduce-scatter.9.cloned.1.call-done = f32[384,512]{0,1:T(8,128)} async-done(((f32[3072,512]{0,1:T(8,128)}), f32[384,512]{0,1:T(8,128)}) %reduce-scatter.9.cloned.1.call-update) | async-done | bytes 786448 | tf_op jit(solution)/shard_map/reduce_scatter | solution.py:47
  673.3 3.3 fusion.14
  679.5 3.1 fusion.6
  682.7 4.5 fusion
  687.1 2.1 fusion.64
  689.7 20.7 %convolution_bitcast_fusion.3 = f32[1536,512]{0,1:T(8,128)} fusion(bf16[3072,512]{1,0:T(8,128)(2,1)} %all-gather.8.cloned.1.call-done, f32[3072,1536]{1,0:T(8,128)} %param.5), kind=kOutput, calls=%fused_computation.4 | convolution fusion | flops 28991029248 | bytes 25165824 | tf_op jit(solution)/shard_map/dot_general | solution.py:19
  710.5 20.9 %convolution_bitcast_fusion.5 = f32[1536,512]{0,1:T(8,128)} fusion(bf16[3072,512]{1,0:T(8,128)(2,1)} %all-gather.4.cloned.1.call-done, f32[3072,1536]{1,0:T(8,128)} %param.5), kind=kOutput, calls=%fused_computation.6 | convolution fusion | flops 28991029248 | bytes 25165824 | tf_op jit(solution)/shard_map/dot_general | solution.py:19
  731.6 21.0 %convolution_bitcast_fusion.4 = f32[1536,512]{0,1:T(8,128)} fusion(bf16[3072,512]{1,0:T(8,128)(2,1)} %all-gather.6.cloned.1.call-done, f32[3072,1536]{1,0:T(8,128)} %param.5), kind=kOutput, calls=%fused_computation.5 | convolution fusion | flops 28991029248 | bytes 25165824 | tf_op jit(solution)/shard_map/dot_general | solution.py:19
  752.6 146.4 %all-reduce.7.cloned.1.call-done = (f32[512,1536]{1,0:T(8,128)}, f32[512,512]{1,0:T(8,128)}, f32[512,1024]{0,1:T(8,128)}) async-done(((f32[512,1536]{1,0:T(8,128)}, f32[512,512]{1,0:T(8,128)}, f32[512,1024]{0,1:T(8,128)}), (f32[512,1536]{1,0:T(8,128)}, f32[512,512]{1,0:T(8,128)}, f32[512,1024]{0,1:T(8,128)})) %all-reduce.7.cloned.1.call-update) | async-done | bytes 6291472 | tf_op jit(solution)/shard_map/psum | solution.py:56
  899.1 2.3 slice.74
  901.4 2.5 copy.65
  903.9 35.1 %reduce-scatter.17.cloned.1.call-done = f32[384,512]{0,1:T(8,128)} async-done(((f32[1536,512]{0,1:T(8,128)}), f32[384,512]{0,1:T(8,128)}) %reduce-scatter.17.cloned.1.call-update) | async-done | bytes 786448 | tf_op jit(solution)/shard_map/reduce_scatter | solution.py:76
  939.0 40.1 %reduce-scatter.13.cloned.1.call-done = f32[384,512]{0,1:T(8,128)} async-done(((f32[1536,512]{0,1:T(8,128)}), f32[384,512]{0,1:T(8,128)}) %reduce-scatter.13.cloned.1.call-update) | async-done | bytes 786448 | tf_op jit(solution)/shard_map/reduce_scatter | solution.py:76
  979.1 4.1 convolution_add_fusion.1
  983.2 36.2 %reduce-scatter.15.cloned.1.call-done = f32[384,512]{0,1:T(8,128)} async-done(((f32[1536,512]{0,1:T(8,128)}), f32[384,512]{0,1:T(8,128)}) %reduce-scatter.15.cloned.1.call-update) | async-done | bytes 786448 | tf_op jit(solution)/shard_map/reduce_scatter | solution.py:76
  1019.4 3.4 fusion.16
  1026.3 3.7 copy.51
  1030.1 3.2 pad_maximum_fusion.1
  1033.2 3.2 copy.50
  1036.5 105.0 %all-reduce.9.cloned.1.call-done = (f32[512,1536]{1,0:T(8,128)}, f32[512,512]{1,0:T(8,128)}, f32[512,1024]{0,1:T(8,128)}) async-done(((f32[512,1536]{1,0:T(8,128)}, f32[512,512]{1,0:T(8,128)}, f32[512,1024]{0,1:T(8,128)}), (f32[512,1536]{1,0:T(8,128)}, f32[512,512]{1,0:T(8,128)}, f32[512,1024]{0,1:T(8,128)})) %all-reduce.9.cloned.1.call-update) | async-done | bytes 6291472 | tf_op jit(solution)/shard_map/psum | solution.py:56
  1141.4 3.6 fusion.34
  1145.0 3.2 bitcast_subtract_fusion.7
  1148.2 1.9 fusion.32
  1152.1 2.0 fusion.13
  1157.0 3.3 fusion.12
  1160.3 2.3 fusion.20
  1162.6 2.3 fusion.70
  1164.9 2.6 copy.39
  1167.5 5.3 fusion.11
  1172.8 2.0 maximum_bitcast_fusion.1
  1174.7 2.4 copy.49
  1177.2 2.3 maximum_bitcast_fusion.2
  1180.2 5.1 pad_maximum_fusion
  (88 shorter events, 16.7 us)
Async XLA Ops:
  7.2 66.3 %all-gather.8.cloned.1.call-start = ((), (), s32[]{:S(2)}) async-start(), calls=%async_computation.10 | async-start | bytes 3538944 | tf_op jit(solution)/shard_map/all_gather | solution.py:43
  10.6 123.8 %all-gather.4.cloned.1.call-start = ((), (), s32[]{:S(2)}) async-start(), calls=%async_computation.6 | async-start | bytes 3538944 | tf_op jit(solution)/shard_map/all_gather | solution.py:43
  11.4 183.9 %all-gather.6.cloned.1.call-start = ((), (), s32[]{:S(2)}) async-start(), calls=%async_computation.8 | async-start | bytes 3538944 | tf_op jit(solution)/shard_map/all_gather | solution.py:43
  12.1 278.9 %all-reduce.11.cloned.1.call-start = ((), (), s32[]{:S(2)}) async-start(), calls=%async_computation.17 | async-start | bytes 9437184 | tf_op jit(solution)/shard_map/psum | solution.py:11
  198.2 233.5 %reduce-scatter.11.cloned.1.call-start = ((), (), s32[]{:S(2)}) async-start(), calls=%async_computation.11 | async-start | bytes 7077888 | tf_op jit(solution)/shard_map/reduce_scatter | solution.py:47
  313.3 1.4 copy-start.26
  313.3 239.1 %reduce-scatter.7.cloned.1.call-start = ((), (), s32[]{:S(2)}) async-start(), calls=%async_computation.7 | async-start | bytes 7077888 | tf_op jit(solution)/shard_map/reduce_scatter | solution.py:47
  336.5 11.7 copy-start.25
  336.5 336.7 %reduce-scatter.9.cloned.1.call-start = ((), (), s32[]{:S(2)}) async-start(), calls=%async_computation.9 | async-start | bytes 7077888 | tf_op jit(solution)/shard_map/reduce_scatter | solution.py:47
  370.2 182.2 %copy-start = (f32[3,512,512]{2,1,0:T(8,128)S(1)}, f32[3,512,512]{2,1,0:T(8,128)}, u32[]{:S(2)}) copy-start(f32[3,512,512]{2,1,0:T(8,128)} %param.7) | copy-start | bytes 9437188
  370.2 528.9 %all-reduce.7.cloned.1.call-start = ((), (), s32[]{:S(2)}) async-start(), calls=%async_computation.15 | async-start | bytes 12582912 | tf_op jit(solution)/shard_map/psum | solution.py:56
  673.3 3.4 copy-start.23
  673.3 5.3 copy-start.7
  676.6 6.0 copy-start.3
  676.6 2.9 copy-start.22
  678.5 4.1 copy-start.12
  678.5 4.1 copy-start.14
  682.7 4.5 copy-start.21
  689.3 249.7 %reduce-scatter.17.cloned.1.call-start = ((), (), s32[]{:S(2)}) async-start(), calls=%async_computation.14 | async-start | bytes 3932160 | tf_op jit(solution)/shard_map/reduce_scatter | solution.py:76
  710.4 268.7 %reduce-scatter.13.cloned.1.call-start = ((), (), s32[]{:S(2)}) async-start(), calls=%async_computation.12 | async-start | bytes 3932160 | tf_op jit(solution)/shard_map/reduce_scatter | solution.py:76
  731.3 288.1 %reduce-scatter.15.cloned.1.call-start = ((), (), s32[]{:S(2)}) async-start(), calls=%async_computation.13 | async-start | bytes 3932160 | tf_op jit(solution)/shard_map/reduce_scatter | solution.py:76
  752.6 388.8 %all-reduce.9.cloned.1.call-start = ((), (), s32[]{:S(2)}) async-start(), calls=%async_computation.16 | async-start | bytes 12582912 | tf_op jit(solution)/shard_map/psum | solution.py:56
  1019.4 3.4 copy-start.24
  1019.4 5.3 copy-start.13
  1141.4 3.6 copy-start.10
  1141.4 3.6 copy-start.11
  1148.2 3.8 copy-start.1
  1148.2 3.8 copy-start.15
  1148.2 3.8 copy-start.16
  1150.1 12.4 %copy-start.4 = (f32[512,512]{0,1:T(8,128)}, f32[512,512]{0,1:T(8,128)S(1)}, u32[]{:S(2)}) copy-start(f32[512,512]{0,1:T(8,128)S(1)} %fusion.32) | copy-start | bytes 3145732
  1152.1 4.9 copy-start.6
  1154.1 1.0 copy-start.8
  1156.9 5.6 copy-start.5
  1167.5 5.3 copy-start.9
  1167.5 5.3 copy-start.19
  1167.5 5.3 copy-start.20
  1177.1 2.4 copy-start.2
  1177.1 2.5 copy-start.17
  1177.2 2.8 copy-start.18
Sparse Core Ops, SparseCore 0:
  10.7 62.7 all-gather.7
  75.7 58.6 all-gather.3
  136.6 58.6 all-gather.5
  198.3 92.7 all-reduce.10
  313.4 118.1 reduce-scatter.10
  435.1 117.2 reduce-scatter.6
  556.0 117.2 reduce-scatter.8
  689.4 209.6 all-reduce.6
  902.2 36.7 reduce-scatter.16
  941.4 37.7 reduce-scatter.12
  981.7 37.7 reduce-scatter.14
  1021.8 119.6 all-reduce.8
